TPU v7x, 512 devices: a whole 4x4x16 slice. The times are simulated.
512 devices in a mesh: tok: 64 (over y_lo, z, core), head: 8 (over y_hi, x).
Axes of the slice: x: 4, y: 4 (y_hi: 2, y_lo: 2; y = y_hi * 2 + y_lo), z: 16, core: 2. Of those that a mesh axis runs over, the one named last changes fastest.
Arguments:
- tokens: bfloat16 [8192, 3072], P('tok', 'head'), may hold values from -6 to 6
- norm_gain: bfloat16 [3072], replicated, may hold values from 0.099609375 to 1.8984375
- w_query: bfloat16 [3072, 3072], P('tok', 'head'), may hold values from -0.3125 to 0.3125
- w_key: bfloat16 [3072, 1024], P('tok', 'head'), may hold values from -0.3125 to 0.3125
- w_value: bfloat16 [3072, 1024], P('tok', 'head'), may hold values from -0.3125 to 0.3125
- w_out: bfloat16 [3072, 3072], P('tok', 'head'), may hold values from -0.109375 to 0.109375
- cache_keys: bfloat16 [64, 512, 1024], P(None, 'tok', 'head')
- cache_values: bfloat16 [64, 512, 1024], P(None, 'tok', 'head'), may hold values from -18 to 18
- lengths: int32 [64], P('tok'), may hold values from 2 to 512, as said below
- page_table: int32 [64, 32], P('tok'), may hold values from 0 to 31, each once within a row
Outputs:
- mixed: bfloat16 [8192, 3072], P('tok', 'head')
- decode_keys: bfloat16 [2048, 16, 1024], P('tok', None, 'head')
- decode_values: bfloat16 [2048, 16, 1024], P('tok', None, 'head')
Inputs may be any that keep to these rules, and one draw needn't show every extreme that they name: lengths are 2 or more, and some request has exactly 512. Each row of page_table names every page slot once.
All inputs are finite; a program needn't handle non-finite values.
Results may differ from a plain program's by a relative error of at most 0.018.
Values may be sent and summed in bfloat16 or wider, within the bound.
A program may use at most 64 MiB of HBM per device.

v0:
```python
import math
import jax
import jax.numpy as jnp
from jax import lax
from jax.sharding import PartitionSpec as P

HD = 128
rope_base = 500000.0
norm_eps = 1e-05


def rotate(values, positions, head_size):
    row_count = values.shape[0]
    shaped = values.reshape(row_count, -1, head_size)
    half_size = head_size // 2
    exponent = jnp.arange(half_size, dtype=jnp.float32) * (2.0 / head_size)
    frequency = jnp.exp(-math.log(rope_base) * exponent)
    angles = positions.astype(jnp.float32)[:, None] * frequency[None, :]
    cosine = jnp.cos(angles)[:, None, :]
    sine_part = jnp.sin(angles)[:, None, :]
    first_half = shaped[:, :, :half_size]
    second_half = shaped[:, :, half_size:]
    turned = jnp.concatenate(
        [
            first_half * cosine - second_half * sine_part,
            second_half * cosine + first_half * sine_part,
        ],
        axis=2,
    )
    return turned.reshape(row_count, -1)


def attend_head(queries, cached_keys, cached_values, span_keys, span_values, live_slots, causal):
    score_scale = 1.0 / math.sqrt(queries.shape[1])
    numbers = (((1,), (1,)), ((), ()))
    cached_scores = (
        lax.dot_general(queries, cached_keys, numbers, preferred_element_type=jnp.float32)
        * score_scale
    )
    span_scores = (
        lax.dot_general(queries, span_keys, numbers, preferred_element_type=jnp.float32)
        * score_scale
    )
    cached_scores = jnp.where(live_slots[None, :], cached_scores, -jnp.inf)
    span_scores = jnp.where(causal, span_scores, -jnp.inf)
    row_max = jnp.maximum(jnp.max(cached_scores, axis=1), jnp.max(span_scores, axis=1))[:, None]
    cached_exp = jnp.exp(cached_scores - row_max)
    span_exp = jnp.exp(span_scores - row_max)
    row_total = jnp.sum(cached_exp, axis=1, keepdims=True) + jnp.sum(
        span_exp, axis=1, keepdims=True
    )
    cached_weights = (cached_exp / row_total).astype(jnp.bfloat16)
    span_weights = (span_exp / row_total).astype(jnp.bfloat16)
    head_out = jnp.dot(cached_weights, cached_values, preferred_element_type=jnp.float32)
    head_out = head_out + jnp.dot(span_weights, span_values, preferred_element_type=jnp.float32)
    return head_out.astype(jnp.bfloat16)


def shards(
    tokens, norm_gain, w_query, w_key, w_value, w_out, cache_keys, cache_values, lengths, page_table
):
    full_rows = lax.all_gather(tokens, "head", axis=1, tiled=True)
    span_len = full_rows.shape[0]
    as_float = full_rows.astype(jnp.float32)
    mean_square = jnp.mean(as_float * as_float, axis=1, keepdims=True)
    normed = (
        as_float * lax.rsqrt(mean_square + norm_eps) * norm_gain.astype(jnp.float32)[None, :]
    ).astype(jnp.bfloat16)

    def add_rows(weight_rows):
        return jnp.dot(normed, weight_rows, preferred_element_type=jnp.float32)

    query_sum = add_rows(lax.all_gather(w_query, "tok", axis=0, tiled=True))
    key_sum = add_rows(lax.all_gather(w_key, "tok", axis=0, tiled=True))
    value_sum = add_rows(lax.all_gather(w_value, "tok", axis=0, tiled=True))
    length = lengths[0]
    positions = length + jnp.arange(span_len, dtype=jnp.int32)
    queries = rotate(query_sum, positions, HD).astype(jnp.bfloat16)
    key_new = rotate(key_sum, positions, HD).astype(jnp.bfloat16)
    value_new = value_sum.astype(jnp.bfloat16)
    moved_keys, moved_values = (
        lax.all_to_all(cache_keys, "tok", split_axis=0, concat_axis=1, tiled=True),
        lax.all_to_all(cache_values, "tok", split_axis=0, concat_axis=1, tiled=True),
    )
    slot_total = moved_keys.shape[1]
    live_slots = jnp.arange(slot_total, dtype=jnp.int32) < length
    keys_live = jnp.where(live_slots[:, None], moved_keys[0], jnp.zeros_like(moved_keys[0]))
    values_live = jnp.where(live_slots[:, None], moved_values[0], jnp.zeros_like(moved_values[0]))
    slot_count = page_table.shape[1]
    page_keys = keys_live.reshape(slot_count, -1, keys_live.shape[1])
    page_values = values_live.reshape(slot_count, -1, values_live.shape[1])
    decode_keys = jnp.zeros_like(page_keys).at[page_table[0]].set(page_keys)
    decode_values = jnp.zeros_like(page_values).at[page_table[0]].set(page_values)
    token_ids = jnp.arange(span_len, dtype=jnp.int32)
    causal = token_ids[None, :] <= token_ids[:, None]
    local_heads = queries.shape[1] // HD

    def one_head(head_number):
        head_start = head_number * HD
        return attend_head(
            lax.dynamic_slice_in_dim(queries, head_start, HD, 1),
            keys_live,
            values_live,
            key_new,
            value_new,
            live_slots,
            causal,
        )

    heads_out = lax.map(one_head, jnp.arange(local_heads, dtype=jnp.int32))
    attention = jnp.transpose(heads_out, (1, 0, 2)).reshape(span_len, local_heads * HD)
    partial_out = lax.dot_general(
        attention,
        lax.all_gather(w_out, "tok", axis=0, tiled=True),
        (((1,), (1,)), ((), ())),
        preferred_element_type=jnp.float32,
    )
    mixed = lax.psum_scatter(
        partial_out.astype(jnp.bfloat16), "head", scatter_dimension=1, tiled=True
    )
    return (mixed, decode_keys, decode_values)


def solution(mesh):
    in_specs = (
        P("tok", "head"),
        P(),
        P("tok", "head"),
        P("tok", "head"),
        P("tok", "head"),
        P("tok", "head"),
        P(None, "tok", "head"),
        P(None, "tok", "head"),
        P("tok"),
        P("tok", None),
    )
    out_specs = (P("tok", "head"), P("tok", None, "head"), P("tok", None, "head"))
    return jax.shard_map(shards, mesh=mesh, in_specs=in_specs, out_specs=out_specs, check_vma=False)
```

profile of v0, /device:TPU:2, one launch (start us, length us, event | category | flops | bytes accessed | tf_op | source)
XLA Modules:
  0.0 356.6 jit_solution(9091315769664037303)
XLA Ops:
  7.2 0.7 all-gather.3.cloned.1.call-update
  7.9 17.1 %all-to-all-start = ((bf16[64,8,128]{2,1,0:T(8,128)(2,1)}), bf16[64,8,128]{2,1,0:T(8,128)(2,1)S(1)}, u32[]{:S(2)}, u32[]{:S(2)}) async-start(bf16[64,8,128]{2,1,0:T(8,128)(2,1)} %param.18), calls=%async_computation | async-start | bytes 262144 | tf_op jit(solution)/shard_map/all_to_all | solution.py:82
  25.1 0.7 all-gather.5.cloned.1.call-update
  25.8 36.2 %all_gather.15 = bf16[128,3072]{1,0:T(8,128)(2,1)S(1)} all-gather(bf16[128,384]{1,0:T(8,128)(2,1)} %param.12), channel_id=1, replica_groups=mesh['tok'=64,'head'=8] {'head'}, dimensions={1}, use_global_device_ids=true | all-gather | bytes 884736 | tf_op jit(solution)/shard_map/all_gather | solution.py:62
  62.0 0.2 fusion.17
  62.9 64.6 %all_gather.17 = bf16[3072,128]{1,0:T(8,128)(2,1)S(1)} all-gather(bf16[48,128]{1,0:T(8,128)(2,1)S(1)} %copy-done.2), channel_id=1, replica_groups=mesh['tok'=64,'head'=8] {'tok'}, dimensions={0}, use_global_device_ids=true | all-gather | bytes 798720 | tf_op jit(solution)/shard_map/all_gather | solution.py:74
  127.5 0.5 convolution_bitcast_fusion
  128.3 61.8 %all_gather.18 = bf16[3072,128]{1,0:T(8,128)(2,1)S(1)} all-gather(bf16[48,128]{1,0:T(8,128)(2,1)S(1)} %copy-done.3), channel_id=1, replica_groups=mesh['tok'=64,'head'=8] {'tok'}, dimensions={0}, use_global_device_ids=true | all-gather | bytes 798720 | tf_op jit(solution)/shard_map/all_gather | solution.py:75
  190.1 4.6 %all-to-all-start.1 = ((bf16[64,8,128]{2,1,0:T(8,128)(2,1)}), bf16[64,8,128]{2,1,0:T(8,128)(2,1)S(1)}, u32[]{:S(2)}, u32[]{:S(2)}) async-start(bf16[64,8,128]{2,1,0:T(8,128)(2,1)} %param.19), calls=%async_computation.1 | async-start | bytes 262144 | tf_op jit(solution)/shard_map/all_to_all | solution.py:83
  195.1 0.4 convolution_convert_fusion.1
  195.5 17.0 %all-to-all-done.1 = bf16[64,8,128]{2,1,0:T(8,128)(2,1)S(1)} async-done(((bf16[64,8,128]{2,1,0:T(8,128)(2,1)}), bf16[64,8,128]{2,1,0:T(8,128)(2,1)S(1)}, u32[]{:S(2)}, u32[]{:S(2)}) %all-to-all-start.1) | async-done | bytes 131104 | tf_op jit(solution)/shard_map/all_to_all | solution.py:83
  212.7 2.7 fusion.31
  215.5 9.7 %while.11 = (s32[]{:T(128)}, bf16[3,128,128]{1,2,0:T(8,128)(2,1)S(1)}, s32[3]{0:T(128)S(1)}, bf16[128,384]{0,1:T(8,128)(2,1)S(1)}, bf16[512,128]{1,0:T(8,128)(2,...) while((s32[]{:T(128)}, ...), condition=%wide.region_6.7_spmd.clone, body=%wide.region_1.6_spmd.clone.sunk | while | flops 42647812 | bytes 1680583 | solution.py:110
  215.5 0.6 dynamic_slice.22
  216.8 0.7 iota_compare_fusion.4
  217.4 0.3 fusion.58
  218.1 0.3 fusion.62
  218.8 0.6 dynamic_slice.22
  220.0 0.7 iota_compare_fusion.4
  220.7 0.3 fusion.58
  221.4 0.3 fusion.62
  222.0 0.6 dynamic_slice.22
  223.2 0.7 iota_compare_fusion.4
  223.9 0.3 fusion.58
  224.6 0.3 fusion.62
  225.2 35.4 %all-gather.5.cloned.1.call-done = bf16[3072,384]{1,0:T(8,128)(2,1)} async-done(((bf16[48,384]{1,0:T(8,128)(2,1)}), bf16[3072,384]{1,0:T(8,128)(2,1)}) %all-gather.5.cloned.1.call-update) | async-done | bytes 2359312 | tf_op jit(solution)/shard_map/all_gather | solution.py:114
  260.7 2.6 convolution_convert_fusion
  263.3 1.2 copy.23
  264.7 1.5 scatter_fusion
  266.2 1.5 scatter_fusion.1
  267.7 80.7 %reduce-scatter.4.cloned.1.call-done = bf16[384,128]{1,0:T(8,128)(2,1)} async-done(((bf16[3072,128]{1,0:T(8,128)(2,1)}), bf16[384,128]{1,0:T(8,128)(2,1)}) %reduce-scatter.4.cloned.1.call-update) | async-done | bytes 98320
  348.5 1.6 copy.24
  (61 shorter events, 3.3 us)
Async XLA Ops:
  7.2 55.1 %copy-start.4 = (bf16[3072]{0:T(1024)(128)(2,1)S(1)}, bf16[3072]{0:T(1024)(128)(2,1)}, u32[]{:S(2)}) copy-start(bf16[3072]{0:T(1024)(128)(2,1)} %param.13) | copy-start | bytes 18436
  7.2 55.8 %copy-start.2 = (bf16[48,128]{1,0:T(8,128)(2,1)S(1)}, bf16[48,128]{1,0:T(8,128)(2,1)}, u32[]{:S(2)}) copy-start(bf16[48,128]{1,0:T(8,128)(2,1)} %param.15) | copy-start | bytes 36868
  7.2 205.5 %all-gather.3.cloned.1.call-start = ((), (), s32[]{:S(2)}) async-start(), calls=%async_computation.3 | async-start | bytes 2396160 | tf_op jit(solution)/shard_map/all_gather | solution.py:73
  7.9 182.1 %all-to-all-start = ((bf16[64,8,128]{2,1,0:T(8,128)(2,1)}), bf16[64,8,128]{2,1,0:T(8,128)(2,1)S(1)}, u32[]{:S(2)}, u32[]{:S(2)}) async-start(bf16[64,8,128]{2,1,0:T(8,128)(2,1)} %param.18), calls=%async_computation | async-start | bytes 262144 | tf_op jit(solution)/shard_map/all_to_all | solution.py:82
  25.1 235.6 %all-gather.5.cloned.1.call-start = ((), (), s32[]{:S(2)}) async-start(), calls=%async_computation.4 | async-start | bytes 2396160 | tf_op jit(solution)/shard_map/all_gather | solution.py:114
  62.2 66.0 %copy-start.3 = (bf16[48,128]{1,0:T(8,128)(2,1)S(1)}, bf16[48,128]{1,0:T(8,128)(2,1)}, u32[]{:S(2)}) copy-start(bf16[48,128]{1,0:T(8,128)(2,1)} %param.16) | copy-start | bytes 36868
  190.1 22.5 %all-to-all-start.1 = ((bf16[64,8,128]{2,1,0:T(8,128)(2,1)}), bf16[64,8,128]{2,1,0:T(8,128)(2,1)S(1)}, u32[]{:S(2)}, u32[]{:S(2)}) async-start(bf16[64,8,128]{2,1,0:T(8,128)(2,1)} %param.19), calls=%async_computation.1 | async-start | bytes 262144 | tf_op jit(solution)/shard_map/all_to_all | solution.py:83
  194.7 153.8 %reduce-scatter.4.cloned.1.call-start = ((), (), s32[]{:S(2)}) async-start(), calls=%async_computation.5 | async-start | bytes 884736
  263.2 1.2 copy-start.5
  266.2 83.9 %copy-start.1 = (bf16[32,16,128]{2,1,0:T(8,128)(2,1)}, bf16[32,16,128]{2,1,0:T(8,128)(2,1)S(1)}, u32[]{:S(2)}) copy-start(bf16[32,16,128]{2,1,0:T(8,128)(2,1)S(1)} %scatter_fusion) | copy-start | bytes 393220
  267.7 82.4 %copy-start = (bf16[32,16,128]{2,1,0:T(8,128)(2,1)}, bf16[32,16,128]{2,1,0:T(8,128)(2,1)S(1)}, u32[]{:S(2)}) copy-start(bf16[32,16,128]{2,1,0:T(8,128)(2,1)S(1)} %scatter_fusion.1) | copy-start | bytes 393220
Sparse Core Ops, SparseCore 0:
  10.2 127.4 all-gather.2
  139.8 120.8 all-gather.4
  265.2 83.2 reduce-scatter.3
where the time goes:
time: 357 us
  blocking collectives  163 us (46%)
  waiting for transfers between devices  135 us (38%)
  starting transfers between devices  21.9 us (6%)
  between operations  14.7 us (4%)
  matrix products  9 us (3%)
  local copies, waits for them, and re-layouts  8.13 us (2%)
  other arithmetic  3.71 us (1%)
    unnamed x4, waiting for transfers between devices  82.1 us
    all_gather x1, blocking collectives, shards(): key_sum = add_rows(lax.all_gather(w_key, 'tok', axis=0, tiled=True))  64.6 us
    all_gather x1, blocking collectives, shards(): value_sum = add_rows(lax.all_gather(w_value, 'tok', axis=0, tiled=True))  61.8 us
    all_gather x1, blocking collectives, shards(): full_rows = lax.all_gather(tokens, 'head', axis=1, tiled=True)  36.2 us
    all_gather x1, waiting for transfers between devices, shards(): lax.all_gather(w_out, 'tok', axis=0, tiled=True)  35.4 us
    all_to_all x1, starting transfers between devices, shards(): lax.all_to_all(cache_keys, 'tok', split_axis=0, concat_axis=1, tiled=True)  17.1 us
    all_to_all x1, waiting for transfers between devices, shards(): lax.all_to_all(cache_values, 'tok', split_axis=0, concat_axis=1, tiled=True)  17 us
  transfers between devices with their start and end apart: 5, of which 3 were waited for; matrix products, arithmetic and copies ran while one was open for 4% of the time, Pallas kernels for 0%

commit v1 on v0

--- a/solution.py
+++ b/solution.py
@@ -111,7 +111,9 @@
     attention = jnp.transpose(heads_out, (1, 0, 2)).reshape(span_len, local_heads * HD)
     partial_out = lax.dot_general(
         attention,
-        lax.all_gather(w_out, "tok", axis=0, tiled=True),
+        jnp.concatenate(
+            lax.all_to_all(jnp.stack([w_out] * lax.axis_size("tok")), "tok", 0, 0), axis=0
+        ),
         (((1,), (1,)), ((), ())),
         preferred_element_type=jnp.float32,
     )

time: 357 us -> 416 us (1.17)
  blocking collectives: 163 us -> 285 us
  waiting for transfers between devices: 135 us -> 76.9 us
  starting transfers between devices: 21.9 us -> 4.91 us
  local copies, waits for them, and re-layouts: 8.13 us -> 13 us
  matrix products: 9 us -> 13.8 us
    all_gather x1, blocking collectives: 64.6 us -> 131 us  [shards(): key_sum = add_rows(lax.all_gather(w_key, 'tok', axis=0, tiled=True))]
    all_to_all x0 -> x2, blocking collectives: none -> 55.9 us  [the longest x1 34.2 us: shards(): lax.all_to_all(cache_keys, 'tok', split_axis=0, concat_axis=1, tiled=True)]
    all_gather x1 -> x0, waiting for transfers between devices: 35.4 us -> none  [shards(): lax.all_gather(w_out, 'tok', axis=0, tiled=True)]
    all_to_all x2 -> x1, waiting for transfers between devices: 17 us -> 0.01 us  [shards(): lax.all_to_all(jnp.stack([w_out] * lax.axis_size('tok')), 'tok', 0, 0)]
    all_to_all x2 -> x1, starting transfers between devices: 21.7 us -> 4.83 us  [shards(): lax.all_to_all(jnp.stack([w_out] * lax.axis_size('tok')), 'tok', 0, 0)]
    unnamed x4 -> x3, waiting for transfers between devices: 82.1 us -> 76.9 us
  transfers between devices with their start and end apart: 5 -> 3, of which waited for: 3 -> 1; matrix products, arithmetic and copies ran while one was open for 4% -> 6% of each run, Pallas kernels for 0% -> 0%
where the time goes in v1:
time: 416 us; the launch traced here: 415 us
  blocking collectives  285 us (69%)
  waiting for transfers between devices  76.9 us (18%)
  between operations  14.9 us (4%)
  matrix products  13.8 us (3%)
  local copies, waits for them, and re-layouts  13 us (3%)
  other arithmetic  4.98 us (1%)
  starting transfers between devices  4.91 us (1%)
    all_gather x1, blocking collectives, shards(): key_sum = add_rows(lax.all_gather(w_key, 'tok', axis=0, tiled=True))  131 us
    unnamed x3, waiting for transfers between devices  76.9 us
    all_gather x1, blocking collectives, shards(): value_sum = add_rows(lax.all_gather(w_value, 'tok', axis=0, tiled=True))  61.7 us
    all_gather x1, blocking collectives, shards(): full_rows = lax.all_gather(tokens, 'head', axis=1, tiled=True)  36.4 us
    all_to_all x1, blocking collectives, shards(): lax.all_to_all(cache_keys, 'tok', split_axis=0, concat_axis=1, tiled=True)  34.2 us
    all_to_all x1, blocking collectives, shards(): lax.all_to_all(cache_values, 'tok', split_axis=0, concat_axis=1, tiled=True)  21.7 us
  transfers between devices with their start and end apart: 3, of which 1 were waited for; matrix products, arithmetic and copies ran while one was open for 6% of the time, Pallas kernels for 0%

profile of v1, /device:TPU:2, one launch (start us, length us, event | category | flops | bytes accessed | tf_op | source)
XLA Modules:
  0.0 415.2 jit_solution(937361261031181933)
XLA Ops:
  7.2 34.2 %all_to_all.23 = bf16[64,8,128]{2,1,0:T(8,128)(2,1)S(1)} all-to-all(bf16[64,8,128]{2,1,0:T(8,128)(2,1)} %param.18), channel_id=1, replica_groups=mesh['tok'=64,'head'=8] {'tok'}, dimensions={0} | all-to-all | bytes 262144 | tf_op jit(solution)/shard_map/all_to_all | solution.py:82
  41.4 21.7 %all_to_all.24 = bf16[64,8,128]{2,1,0:T(8,128)(2,1)S(1)} all-to-all(bf16[64,8,128]{2,1,0:T(8,128)(2,1)} %param.19), channel_id=1, replica_groups=mesh['tok'=64,'head'=8] {'tok'}, dimensions={0} | all-to-all | bytes 262144 | tf_op jit(solution)/shard_map/all_to_all | solution.py:83
  63.1 2.4 stack.2
  65.5 4.8 %all-to-all-start.2 = ((bf16[64,48,384]{2,1,0:T(8,128)(2,1)}), bf16[64,48,384]{2,1,0:T(8,128)(2,1)S(1)}, u32[]{:S(2)}, u32[]{:S(2)}) async-start(bf16[64,48,384]{2,1,0:T(8,128)(2,1)} %stack.2), calls=%async_computation.2 | async-start | bytes 4718592 | tf_op jit(solution)/shard_map/all_to_all | solution.py:115
  70.4 0.7 all-gather.2.cloned.1.call-update
  71.8 36.4 %all_gather.12 = bf16[128,3072]{1,0:T(8,128)(2,1)S(1)} all-gather(bf16[128,384]{1,0:T(8,128)(2,1)S(1)} %copy-done.4), channel_id=1, replica_groups=mesh['tok'=64,'head'=8] {'head'}, dimensions={1}, use_global_device_ids=true | all-gather | bytes 884736 | tf_op jit(solution)/shard_map/all_gather | solution.py:62
  108.5 130.6 %all_gather.14 = bf16[3072,128]{1,0:T(8,128)(2,1)S(1)} all-gather(bf16[48,128]{1,0:T(8,128)(2,1)S(1)} %copy-done.5), channel_id=1, replica_groups=mesh['tok'=64,'head'=8] {'tok'}, dimensions={0}, use_global_device_ids=true | all-gather | bytes 798720 | tf_op jit(solution)/shard_map/all_gather | solution.py:74
  239.8 0.7 copy.20
  240.5 0.8 multiply_cosine_fusion.1
  241.3 61.7 %all_gather.15 = bf16[3072,128]{1,0:T(8,128)(2,1)S(1)} all-gather(bf16[48,128]{1,0:T(8,128)(2,1)S(1)} %copy-done.6), channel_id=1, replica_groups=mesh['tok'=64,'head'=8] {'tok'}, dimensions={0}, use_global_device_ids=true | all-gather | bytes 798720 | tf_op jit(solution)/shard_map/all_gather | solution.py:75
  303.0 1.0 convolution_convert_fusion.1
  304.0 0.8 bitcast_select_fusion.2
  304.8 2.7 fusion.31
  307.7 16.5 %while.11 = (s32[]{:T(128)}, bf16[3,128,128]{1,2,0:T(8,128)(2,1)}, s32[3]{0:T(128)S(1)}, bf16[128,384]{0,1:T(8,128)(2,1)S(1)}, bf16[512,128]{1,0:T(8,128)(2,1)S(...) while((s32[]{:T(128)}, bf16[3,128,128]{1,2,0:T(8,128)(2,1)}, ...), condition=%wide.region_6.7_spmd.clone, body=%wide.region_1.6_spmd.clone.sunk | while | flops 42647812 | bytes 1811691 | solution.py:110
  309.0 0.7 iota_compare_fusion.4
  309.6 0.9 fusion.59
  311.1 1.2 fusion.62
  312.6 0.6 constant_dynamic-update-slice_fusion.2
  314.5 0.7 iota_compare_fusion.4
  315.1 0.9 fusion.59
  316.6 1.2 fusion.62
  318.1 0.6 constant_dynamic-update-slice_fusion.2
  320.0 0.7 iota_compare_fusion.4
  320.6 0.9 fusion.59
  322.1 1.2 fusion.62
  323.6 0.6 constant_dynamic-update-slice_fusion.2
  324.2 1.8 convolution_convert_fusion
  326.0 1.2 copy.23
  327.4 1.5 scatter_fusion.1
  329.0 1.5 scatter_fusion
  330.5 76.2 %reduce-scatter.4.cloned.1.call-done = bf16[384,128]{1,0:T(8,128)(2,1)} async-done(((bf16[3072,128]{1,0:T(8,128)(2,1)}), bf16[384,128]{1,0:T(8,128)(2,1)}) %reduce-scatter.4.cloned.1.call-update) | async-done | bytes 98320
  406.7 1.6 copy.24
  (71 shorter events, 5.7 us)
Async XLA Ops:
  65.5 6.3 %copy-start.7 = (bf16[3072]{0:T(1024)(128)(2,1)S(1)}, bf16[3072]{0:T(1024)(128)(2,1)}, u32[]{:S(2)}) copy-start(bf16[3072]{0:T(1024)(128)(2,1)} %param.13) | copy-start | bytes 18436
  65.5 6.3 %copy-start.4 = (bf16[128,384]{1,0:T(8,128)(2,1)S(1)}, bf16[128,384]{1,0:T(8,128)(2,1)}, u32[]{:S(2)}) copy-start(bf16[128,384]{1,0:T(8,128)(2,1)} %param.12) | copy-start | bytes 294916
  65.5 258.7 %all-to-all-start.2 = ((bf16[64,48,384]{2,1,0:T(8,128)(2,1)}), bf16[64,48,384]{2,1,0:T(8,128)(2,1)S(1)}, u32[]{:S(2)}, u32[]{:S(2)}) async-start(bf16[64,48,384]{2,1,0:T(8,128)(2,1)} %stack.2), calls=%async_computation.2 | async-start | bytes 4718592 | tf_op jit(solution)/shard_map/all_to_all | solution.py:115
  70.3 38.1 %copy-start.5 = (bf16[48,128]{1,0:T(8,128)(2,1)S(1)}, bf16[48,128]{1,0:T(8,128)(2,1)}, u32[]{:S(2)}) copy-start(bf16[48,128]{1,0:T(8,128)(2,1)} %param.15) | copy-start | bytes 36868
  70.3 234.5 %all-gather.2.cloned.1.call-start = ((), (), s32[]{:S(2)}) async-start(), calls=%async_computation.4 | async-start | bytes 2396160 | tf_op jit(solution)/shard_map/all_gather | solution.py:73
  71.1 335.6 %reduce-scatter.4.cloned.1.call-start = ((), (), s32[]{:S(2)}) async-start(), calls=%async_computation.5 | async-start | bytes 884736
  108.4 132.9 %copy-start.6 = (bf16[48,128]{1,0:T(8,128)(2,1)S(1)}, bf16[48,128]{1,0:T(8,128)(2,1)}, u32[]{:S(2)}) copy-start(bf16[48,128]{1,0:T(8,128)(2,1)} %param.16) | copy-start | bytes 36868
  304.8 2.8 copy-start.2
  304.8 2.8 copy-start.3
  307.7 4.6 %copy-start.9 = (bf16[128,128]{1,0:T(8,128)(2,1)S(1)}, bf16[128,128]{1,0:T(8,128)(2,1)}, u32[]{:S(2)}) copy-start(bf16[128,128]{1,0:T(8,128)(2,1)} %get-tuple-element.233) | copy-start | bytes 98308 | tf_op jit(solution)/shard_map/while
  313.2 4.5 %copy-start.9 = (bf16[128,128]{1,0:T(8,128)(2,1)S(1)}, bf16[128,128]{1,0:T(8,128)(2,1)}, u32[]{:S(2)}) copy-start(bf16[128,128]{1,0:T(8,128)(2,1)} %get-tuple-element.233) | copy-start | bytes 98308 | tf_op jit(solution)/shard_map/while
  318.7 4.5 %copy-start.9 = (bf16[128,128]{1,0:T(8,128)(2,1)S(1)}, bf16[128,128]{1,0:T(8,128)(2,1)}, u32[]{:S(2)}) copy-start(bf16[128,128]{1,0:T(8,128)(2,1)} %get-tuple-element.233) | copy-start | bytes 98308 | tf_op jit(solution)/shard_map/while
  326.0 1.2 copy-start.8
  328.9 79.4 %copy-start.1 = (bf16[32,16,128]{2,1,0:T(8,128)(2,1)}, bf16[32,16,128]{2,1,0:T(8,128)(2,1)S(1)}, u32[]{:S(2)}) copy-start(bf16[32,16,128]{2,1,0:T(8,128)(2,1)S(1)} %scatter_fusion.1) | copy-start | bytes 393220
  330.5 77.9 %copy-start = (bf16[32,16,128]{2,1,0:T(8,128)(2,1)}, bf16[32,16,128]{2,1,0:T(8,128)(2,1)S(1)}, u32[]{:S(2)}) copy-start(bf16[32,16,128]{2,1,0:T(8,128)(2,1)S(1)} %scatter_fusion) | copy-start | bytes 393220
Sparse Core Ops, SparseCore 0:
  73.3 151.9 all-gather.1
  327.3 79.3 reduce-scatter.3
